TPU v7x, 512 devices: a whole 4x8x8 slice. The times are simulated.
512 devices in a mesh: leaf: 32 (over y, x), col: 16 (over z, core).
Axes of the slice: x: 4, y: 8, z: 8, core: 2. Of those that a mesh axis runs over, the one named last changes fastest.
Arguments:
- points: float32 [3, 262144], P(None, ('leaf', 'col'))
- point_ids: int32 [262144], P(('leaf', 'col')), may hold values from 0 to 1048575, as said below
- signs: int32 [262144], P(('leaf', 'col')), may hold values from 0 to 1
- hadamard_sample_rows: int32 [512], replicated, may hold values from 0 to 1048575, as said below
- samples: bfloat16 [262144, 512], P(('leaf', 'col')), may hold values from -6 to 6
- skeleton: int32 [60, 128], replicated, may hold values from 0 to 8191, as said below
- ranks: int32 [60], replicated, may hold values from 64 to 128, as said below
Outputs:
- leaf_basis: bfloat16 [262144, 128], P(('leaf', 'col'))
- top_sample: float32 [512, 512], P('leaf', 'col')
- top_omega: float32 [512, 512], P('leaf', 'col')
Inputs may be any that keep to these rules, and one draw needn't show every extreme that they name: `point_ids`: increasing and distinct; the first is 0 and the last 1048575. `hadamard_sample_rows`: increasing and distinct; the first is 0 and the last 1048575. `skeleton`: each row holds distinct indices; in the first 32 rows (leaves) they are below 8192, in the others below 256; entry i of a leaf row lies in [i * 64, (i + 1) * 64). `ranks`: some node has rank 128 and some other node rank 128 / 2.
All inputs are finite; a program needn't handle non-finite values.
Results may differ from a plain program's by a relative error of at most 0.0018.
Values sent between devices are 32-bit elements; how exact they have to be, the bound alone decides.
A program may use at most 64 MiB of HBM per device.

v0:
```python
import jax
import jax.numpy as jnp
from jax import lax
from jax.sharding import PartitionSpec as P

NTOTAL = 1048576
KERNEL_SCALE = 1.0
OMEGA_UNIT = 0.0625
RIDGE = 0.25
HIGH = lax.Precision.HIGHEST


def swapped(value, axis, bit):
    mask = 2**bit
    pairs = [(source, source ^ mask) for source in range(lax.axis_size(axis))]
    return lax.ppermute(value, axis, pairs)


def omega_rows(tags, hadamard_sample_rows, bit_count):
    powers = jnp.array([1 << shift for shift in range(bit_count)], dtype=jnp.int32)
    row_bits = (tags[0][:, None] // powers[None, :] % 2).astype(jnp.float32)
    col_bits = (hadamard_sample_rows[None, :] // powers[:, None] % 2).astype(jnp.float32)
    counted = jnp.dot(row_bits, col_bits, precision=HIGH)
    parity = counted - 2.0 * jnp.floor(0.5 * counted)
    flips = (2 * tags[1] - 1).astype(jnp.float32)
    return (1.0 - 2.0 * parity) * flips[:, None] * OMEGA_UNIT


def kernel_tile(left, right):
    squared_distance = jnp.zeros((left.shape[1], right.shape[1]), jnp.float32)
    for axis_k in range(3):
        offset = left[axis_k][:, None] - right[axis_k][None, :]
        squared_distance = squared_distance + offset * offset
    return jnp.exp(-KERNEL_SCALE * squared_distance)


def ridge_fit(picked, gram, rank):
    shift = RIDGE * jnp.trace(gram) / rank.astype(jnp.float32) + 1e-06
    ident = jnp.eye(gram.shape[0], dtype=jnp.float32)
    factor = jnp.linalg.cholesky(gram + shift * ident)
    return jax.scipy.linalg.cho_solve((factor, True), picked)


def local(points, point_ids, signs, hadamard_sample_rows, samples, skeleton, ranks):
    leaf_count = lax.axis_size("leaf")
    col_count = lax.axis_size("col")
    leaf_pos = lax.axis_index("leaf")
    col_pos = lax.axis_index("col")
    rows = points.shape[1]
    width = samples.shape[1]
    rank_limit = skeleton.shape[1]
    bit_count = NTOTAL.bit_length() - 1
    tags = jnp.stack([point_ids, signs])
    own_omega = omega_rows(tags, hadamard_sample_rows, bit_count)
    distant_points = lax.all_gather(points, "col", axis=1, tiled=True)
    far_tags = lax.all_gather(tags, "col", axis=1, tiled=True)
    block_omega = omega_rows(far_tags, hadamard_sample_rows, bit_count).astype(jnp.bfloat16)
    tile = kernel_tile(points, distant_points).astype(jnp.bfloat16)
    near = jnp.dot(tile, block_omega, preferred_element_type=jnp.float32)
    residue = samples.astype(jnp.float32) - near
    positions = jnp.arange(rank_limit, dtype=jnp.int32)
    leaf_skel = skeleton[leaf_pos] - col_pos * rows
    leaf_rank = ranks[leaf_pos]
    keep = (positions < leaf_rank).astype(jnp.float32)
    chooser = (leaf_skel[:, None] == jnp.arange(rows, dtype=jnp.int32)[None, :]).astype(jnp.float32)
    part_picked = jnp.dot(chooser, residue, precision=HIGH) * keep[:, None]
    part_spots = jnp.dot(points, chooser.T, precision=HIGH)
    picked, spots = lax.psum((part_picked, part_spots), "col")
    gram = jnp.dot(picked, picked.T, precision=HIGH)
    fitted = ridge_fit(picked, gram, leaf_rank)
    basis = jnp.dot(residue, fitted.T, precision=HIGH)
    projected = lax.psum(jnp.dot(basis.T, own_omega, precision=HIGH), "col")
    leaf_basis = basis.astype(jnp.bfloat16)
    span = width // col_count
    base = 0
    for level in range(1, 4):
        child_base = base
        base = base + (leaf_count >> level - 1)
        sibling_selected, other_proj, other_spots = swapped(
            (picked, projected, spots), "leaf", level - 1
        )
        is_left = leaf_pos // (1 << level - 1) % 2 == 0
        left_picked = jnp.where(is_left, picked, sibling_selected)
        right_picked = jnp.where(is_left, sibling_selected, picked)
        left_proj = jnp.where(is_left, projected, other_proj)
        right_proj = jnp.where(is_left, other_proj, projected)
        left_positions = jnp.where(is_left, spots, other_spots)
        right_spots = jnp.where(is_left, other_spots, spots)
        pair_index = leaf_pos // (1 << level)
        left_keep = (positions < ranks[child_base + 2 * pair_index]).astype(jnp.float32)
        right_keep = (positions < ranks[child_base + 2 * pair_index + 1]).astype(jnp.float32)
        cross = kernel_tile(left_positions, right_spots)
        upper = (left_picked - jnp.dot(cross, right_proj, precision=HIGH)) * left_keep[:, None]
        lower = (right_picked - jnp.dot(cross.T, left_proj, precision=HIGH)) * right_keep[:, None]
        candidates = jnp.concatenate([upper, lower], 0)
        stacked = jnp.concatenate([left_proj, right_proj], 0)
        cand_spots = jnp.concatenate([left_positions, right_spots], 1)
        node_skel = skeleton[base + pair_index]
        node_rank = ranks[base + pair_index]
        node_keep = (positions < node_rank).astype(jnp.float32)
        selector = (
            node_skel[:, None] == jnp.arange(2 * rank_limit, dtype=jnp.int32)[None, :]
        ).astype(jnp.float32)
        new_picked = jnp.dot(selector, candidates, precision=HIGH) * node_keep[:, None]
        new_spots = jnp.dot(cand_spots, selector.T, precision=HIGH)
        gram = jnp.dot(new_picked, new_picked.T, precision=HIGH)
        fitted = ridge_fit(new_picked, gram, node_rank)
        parent_basis = jnp.dot(candidates, fitted.T, precision=HIGH)
        projected = jnp.dot(parent_basis.T, stacked, precision=HIGH)
        picked = new_picked
        spots = new_spots
    picked = lax.dynamic_slice_in_dim(picked, col_pos * span, span, 1)
    projected = lax.dynamic_slice_in_dim(projected, col_pos * span, span, 1)
    share = rank_limit // 8
    top_sample = lax.dynamic_slice_in_dim(picked, leaf_pos % 8 * share, share, 0)
    top_omega = lax.dynamic_slice_in_dim(projected, leaf_pos % 8 * share, share, 0)
    return (leaf_basis, top_sample, top_omega)


def solution(mesh):
    placed = (
        P(None, ("leaf", "col")),
        P(("leaf", "col")),
        P(("leaf", "col")),
        P(),
        P(("leaf", "col"), None),
        P(),
        P(),
    )
    return jax.shard_map(
        local,
        mesh=mesh,
        in_specs=placed,
        out_specs=(P(("leaf", "col"), None), P("leaf", "col"), P("leaf", "col")),
        check_vma=False,
    )
```

profile of v0, /device:TPU:2, one launch (start us, length us, event | category | flops | bytes accessed | tf_op | source)
XLA Modules:
  0.0 488.6 jit_solution(7445075124836231805)
XLA Ops:
  7.2 23.8 %all_gather.6 = f32[3,8192]{1,0:T(4,128)S(1)} all-gather(f32[3,512]{1,0:T(4,128)} %param.14), channel_id=1, replica_groups=mesh['leaf'=32,'col'=16] {'col'}, dimensions={1}, use_global_device_ids=true | all-gather | bytes 104448 | tf_op jit(solution)/shard_map/all_gather | solution.py:55
  31.0 0.8 fusion.198
  31.8 0.7 pad_add_fusion
  32.5 14.6 %all_gather.7 = s32[2,8192]{1,0:T(2,128)S(1)} all-gather(s32[2,512]{1,0:T(2,128)S(1)} %pad_add_fusion), channel_id=1, replica_groups=mesh['leaf'=32,'col'=16] {'col'}, dimensions={1}, use_global_device_ids=true | all-gather | bytes 69632 | tf_op jit(solution)/shard_map/all_gather | solution.py:56
  47.2 0.7 compare_reduce_fusion
  48.0 1.7 fusion.199
  50.4 0.8 fusion.165
  51.2 29.2 %multiply_convert_fusion = bf16[8192,512]{1,0:T(8,128)(2,1)S(1)} fusion(f32[8192]{0:T(1024)S(1)} %bitcast.150, s32[20]{0:T(128)} %constant.260.clone, s32[8192]{0:T(1024)S(1)} %bitcast.146, pred[8192]{0:T(1024)(128)(4,1)S(1)} %sign_compare_fusion, s32[512]{0:T(512)} %param.17, pred[512]{0:T(512)(128)(4,1)S(1)} %compare_reduce_fusion), kind=kOutput, calls=%fused_computation | convolution fusion | flops 1047515136 | bytes 8464976 | tf_op jit(solution)/shard_map/dot_general | solution.py:23
  80.5 6.7 %fusion.8 = f32[512,512]{1,0:T(8,128)S(1)} fusion(bf16[8192,512]{1,0:T(8,128)(2,1)S(1)} %multiply_convert_fusion, f32[8192]{0:T(1024)S(1)} %bitcast.148, f32[512]{0:T(512)S(1)} %bitcast.156, f32[8192]{0:T(1024)S(1)} %bitcast.149, f32[512]{0:T(512)S(1)} %bitcast.155, f32[8192]{0:T(1024)S(1)} %bitcast.147, f32[512]{0:T(512)S(1)} %bitcast.154, ...), kind=kOutput, calls=%fused_computation.10 | convolution fusion | flops 4337434624 | bytes 10065920 | tf_op jit(solution)/shard_map/dot_general | solution.py:59
  87.2 1.2 convolution_multiply_fusion.3
  88.8 25.2 %psum.22 = f32[3,128]{1,0:T(4,128)S(1)} all-reduce(f32[3,128]{1,0:T(4,128)S(1)} %convolution_bitcast_fusion), channel_id=1, replica_groups=mesh['leaf'=32,'col'=16] {'col'}, use_global_device_ids=true, to_apply=%region_4.8 | all-reduce | flops 384 | bytes 3072 | tf_op jit(solution)/shard_map/psum | solution.py:68
  114.0 2.8 collective-permute-start.1
  119.5 4.1 fusion.54
  124.1 0.7 compare_convert_fusion.4
  129.5 72.7 %all-reduce.3.cloned.1.call-done = f32[128,512]{1,0:T(8,128)} async-done(((f32[128,512]{1,0:T(8,128)}), f32[128,512]{1,0:T(8,128)}) %all-reduce.3.cloned.1.call-update) | async-done | bytes 262160 | tf_op jit(solution)/shard_map/psum | solution.py:68
  202.1 2.1 select_reduce_fusion.7
  205.0 11.7 %cholesky.74 = f32[128,128]{1,0:T(8,128)S(1)} custom-call(f32[128,128]{1,0:T(8,128)S(1)} %fusion.94), custom_call_target="Cholesky" | custom-call | tf_op jit(solution)/shard_map/jit(cholesky)/cholesky | solution.py:40
  218.1 9.8 %custom-call.10 = f32[1,128,128]{1,2,0:T(8,128)S(1)} custom-call(f32[1,128,128]{2,1,0:T(8,128)S(1)} %fusion.71), custom_call_target="InvertDiagBlocksLowerTriangular" | custom-call | tf_op jit(solution)/shard_map/jit(_cho_solve)/triangular_solve | solution.py:41
  227.9 1.4 fusion.92
  229.7 1.8 fusion.200
  231.5 1.8 fusion.9
  233.5 4.0 collective-permute-start.4
  237.5 111.8 %all-reduce.5.cloned.1.call-done = f32[128,512]{1,0:T(8,128)} async-done(((f32[128,512]{1,0:T(8,128)}), f32[128,512]{1,0:T(8,128)}) %all-reduce.5.cloned.1.call-update) | async-done | bytes 262160 | tf_op jit(solution)/shard_map/psum | solution.py:72
  349.3 2.5 collective-permute-start.2
  351.8 3.4 collective-permute-start
  355.2 5.4 %collective-permute-done.2 = f32[128,512]{1,0:T(8,128)S(1)} collective-permute-done((f32[128,512]{1,0:T(8,128)}, f32[128,512]{1,0:T(8,128)S(1)}, u32[]{:S(2)}, u32[]{:S(2)}) %collective-permute-start.2) | collective-permute-done | bytes 262176 | tf_op jit(solution)/shard_map/ppermute | solution.py:16
  360.6 1.0 broadcast_select_fusion.1
  361.6 3.5 collective-permute-done
  365.2 1.5 subtract_multiply_fusion.4
  367.5 1.0 select_reduce_fusion.6
  369.3 11.7 %cholesky.85 = f32[128,128]{1,0:T(8,128)S(1)} custom-call(f32[128,128]{1,0:T(8,128)S(1)} %fusion.89), custom_call_target="Cholesky" | custom-call | tf_op jit(solution)/shard_map/jit(cholesky)/cholesky | solution.py:40
  382.3 9.8 %custom-call.11 = f32[1,128,128]{1,2,0:T(8,128)S(1)} custom-call(f32[1,128,128]{2,1,0:T(8,128)S(1)} %fusion.72), custom_call_target="InvertDiagBlocksLowerTriangular" | custom-call | tf_op jit(solution)/shard_map/jit(_cho_solve)/triangular_solve | solution.py:41
  394.0 4.0 collective-permute-start.5
  398.0 3.4 collective-permute-start.3
  401.6 3.7 collective-permute-start.7
  405.2 1.3 collective-permute-done.5
  406.6 3.7 collective-permute-done.3
  411.6 1.0 select_reduce_fusion.5
  413.4 11.7 %cholesky.96 = f32[128,128]{1,0:T(8,128)S(1)} custom-call(f32[128,128]{1,0:T(8,128)S(1)} %fusion.84), custom_call_target="Cholesky" | custom-call | tf_op jit(solution)/shard_map/jit(cholesky)/cholesky | solution.py:40
  426.5 9.8 %custom-call.12 = f32[1,128,128]{1,2,0:T(8,128)S(1)} custom-call(f32[1,128,128]{2,1,0:T(8,128)S(1)} %fusion.73), custom_call_target="InvertDiagBlocksLowerTriangular" | custom-call | tf_op jit(solution)/shard_map/jit(_cho_solve)/triangular_solve | solution.py:41
  438.2 3.4 collective-permute-start.8
  441.6 2.7 collective-permute-start.6
  444.3 4.7 collective-permute-done.8
  449.0 3.1 collective-permute-done.6
  453.4 1.0 select_reduce_fusion.4
  455.3 11.7 %cholesky.107 = f32[128,128]{1,0:T(8,128)S(1)} custom-call(f32[128,128]{1,0:T(8,128)S(1)} %fusion.79), custom_call_target="Cholesky" | custom-call | tf_op jit(solution)/shard_map/jit(cholesky)/cholesky | solution.py:40
  468.3 9.8 %custom-call.13 = f32[1,128,128]{1,2,0:T(8,128)S(1)} custom-call(f32[1,128,128]{2,1,0:T(8,128)S(1)} %fusion.74), custom_call_target="InvertDiagBlocksLowerTriangular" | custom-call | tf_op jit(solution)/shard_map/jit(_cho_solve)/triangular_solve | solution.py:41
  480.0 0.7 dynamic_slice.64
  (92 shorter events, 22.5 us)
Async XLA Ops:
  7.2 194.9 %all-reduce.3.cloned.1.call-start = ((), (), s32[]{:S(2)}) async-start(), calls=%async_computation | async-start | bytes 524288 | tf_op jit(solution)/shard_map/psum | solution.py:68
  51.2 29.2 %copy-start.5 = (bf16[512,512]{1,0:T(8,128)(2,1)S(1)}, bf16[512,512]{1,0:T(8,128)(2,1)}, u32[]{:S(2)}) copy-start(bf16[512,512]{1,0:T(8,128)(2,1)} %param.18) | copy-start | bytes 1572868
  80.4 8.1 %copy-start.1 = (f32[3,512]{1,0:T(4,128)S(1)}, f32[3,512]{1,0:T(4,128)}, u32[]{:S(2)}) copy-start(f32[3,512]{1,0:T(4,128)} %param.14) | copy-start | bytes 18436
  80.4 37.1 %copy-start.2 = (s32[512]{0:T(512)S(1)}, s32[512]{0:T(512)}, u32[]{:S(2)}) copy-start(s32[512]{0:T(512)} %param.15) | copy-start | bytes 6148
  80.4 37.1 %copy-start.3 = (s32[512]{0:T(512)S(1)}, s32[512]{0:T(512)}, u32[]{:S(2)}) copy-start(s32[512]{0:T(512)} %param.16) | copy-start | bytes 6148
  80.5 39.0 %copy-start.4 = (s32[512]{0:T(512)S(1)}, s32[512]{0:T(512)}, u32[]{:S(2)}) copy-start(s32[512]{0:T(512)} %param.17) | copy-start | bytes 6148
  80.5 39.0 %copy-start.6 = (s32[20]{0:T(128)S(1)}, s32[20]{0:T(128)}, u32[]{:S(2)}) copy-start(s32[20]{0:T(128)} %constant.260.clone) | copy-start | bytes 244
  88.5 260.9 %all-reduce.5.cloned.1.call-start = ((), (), s32[]{:S(2)}) async-start(), calls=%async_computation.1 | async-start | bytes 524288 | tf_op jit(solution)/shard_map/psum | solution.py:72
  114.0 15.5 %collective-permute-start.1 = (f32[3,128]{1,0:T(4,128)S(1)}, f32[3,128]{1,0:T(4,128)S(1)}, u32[]{:S(2)}, u32[]{:S(2)}) collective-permute-start(f32[3,128]{1,0:T(4,128)S(1)} %psum.22), channel_id=1, source_target_pairs={{0,16},{16,0},{32,48},{48,32},{64,80},{80,64},{96,112},{112,96},{1... | collective-permute-start | bytes 4616 | tf_op jit(solution)/shard_map/ppermute | solution.py:16
  202.1 164.5 %copy-start = (f32[128,512]{1,0:T(8,128)S(1)}, f32[128,512]{1,0:T(8,128)}, u32[]{:S(2)}) copy-start(f32[128,512]{1,0:T(8,128)} %all-reduce.3.cloned.1.call-done) | copy-start | bytes 786436
  233.5 121.7 %collective-permute-start.4 = (f32[3,128]{1,0:T(4,128)S(1)}, f32[3,128]{1,0:T(4,128)S(1)}, u32[]{:S(2)}, u32[]{:S(2)}) collective-permute-start(f32[3,128]{1,0:T(4,128)S(1)} %fusion.66), channel_id=1, source_target_pairs={{0,32},{16,48},{32,0},{48,16},{64,96},{80,112},{96,64},{112,80},{1... | collective-permute-start | bytes 4616 | tf_op jit(solution)/shard_map/ppermute | solution.py:16
  349.3 11.3 %collective-permute-start.2 = (f32[128,512]{1,0:T(8,128)}, f32[128,512]{1,0:T(8,128)S(1)}, u32[]{:S(2)}, u32[]{:S(2)}) collective-permute-start(f32[128,512]{1,0:T(8,128)} %all-reduce.5.cloned.1.call-done), channel_id=1, source_target_pairs={{0,16},{16,0},{32,48},{48,32},{64,80},{80,64},{96,112},{112,96},{1... | collective-permute-start | bytes 786440 | tf_op jit(solution)/shard_map/ppermute | solution.py:16
  351.8 13.3 %collective-permute-start = (f32[128,512]{1,0:T(8,128)}, f32[128,512]{1,0:T(8,128)S(1)}, u32[]{:S(2)}, u32[]{:S(2)}) collective-permute-start(f32[128,512]{1,0:T(8,128)} %all-reduce.3.cloned.1.call-done), channel_id=1, source_target_pairs={{0,16},{16,0},{32,48},{48,32},{64,80},{80,64},{96,112},{112,96},{1... | collective-permute-start | bytes 786440 | tf_op jit(solution)/shard_map/ppermute | solution.py:16
  394.0 12.5 %collective-permute-start.5 = (f32[128,512]{1,0:T(8,128)S(1)}, f32[128,512]{1,0:T(8,128)S(1)}, u32[]{:S(2)}, u32[]{:S(2)}) collective-permute-start(f32[128,512]{1,0:T(8,128)S(1)} %fusion.25), channel_id=1, source_target_pairs={{0,32},{16,48},{32,0},{48,16},{64,96},{80,112},{96,64},{112,80},{1... | collective-permute-start | bytes 786440 | tf_op jit(solution)/shard_map/ppermute | solution.py:16
  398.0 12.3 %collective-permute-start.3 = (f32[128,512]{1,0:T(8,128)S(1)}, f32[128,512]{1,0:T(8,128)S(1)}, u32[]{:S(2)}, u32[]{:S(2)}) collective-permute-start(f32[128,512]{1,0:T(8,128)S(1)} %convolution_multiply_fusion.2), channel_id=1, source_target_pairs={{0,32},{16,48},{32,0},{48,16},{64,96},{80,112},{96,64},{112,80},{1... | collective-permute-start | bytes 786440 | tf_op jit(solution)/shard_map/ppermute | solution.py:16
  401.6 40.0 %collective-permute-start.7 = (f32[3,128]{1,0:T(4,128)S(1)}, f32[3,128]{1,0:T(4,128)S(1)}, u32[]{:S(2)}, u32[]{:S(2)}) collective-permute-start(f32[3,128]{1,0:T(4,128)S(1)} %fusion.67), channel_id=1, source_target_pairs={{0,64},{16,80},{32,96},{48,112},{64,0},{80,16},{96,32},{112,48},{1... | collective-permute-start | bytes 4616 | tf_op jit(solution)/shard_map/ppermute | solution.py:16
  438.2 10.8 %collective-permute-start.8 = (f32[128,512]{1,0:T(8,128)S(1)}, f32[128,512]{1,0:T(8,128)S(1)}, u32[]{:S(2)}, u32[]{:S(2)}) collective-permute-start(f32[128,512]{1,0:T(8,128)S(1)} %fusion.29), channel_id=1, source_target_pairs={{0,64},{16,80},{32,96},{48,112},{64,0},{80,16},{96,32},{112,48},{1... | collective-permute-start | bytes 786440 | tf_op jit(solution)/shard_map/ppermute | solution.py:16
  441.6 10.5 %collective-permute-start.6 = (f32[128,512]{1,0:T(8,128)S(1)}, f32[128,512]{1,0:T(8,128)S(1)}, u32[]{:S(2)}, u32[]{:S(2)}) collective-permute-start(f32[128,512]{1,0:T(8,128)S(1)} %convolution_multiply_fusion.1), channel_id=1, source_target_pairs={{0,64},{16,80},{32,96},{48,112},{64,0},{80,16},{96,32},{112,48},{1... | collective-permute-start | bytes 786440 | tf_op jit(solution)/shard_map/ppermute | solution.py:16
Sparse Core Ops, SparseCore 0:
  88.6 113.4 all-reduce.2
  233.4 115.8 all-reduce.4
where the time goes:
time: 496 us; the launch traced here: 489 us
  waiting for transfers between devices  206 us (42%)
  other arithmetic  101 us (20%)
  blocking collectives  63.6 us (13%)
  matrix products  62.6 us (13%)
  starting transfers between devices  29.9 us (6%)
  between operations  20.8 us (4%)
    psum x1, waiting for transfers between devices, local(): projected = lax.psum(jnp.dot(basis.T, own_omega, precision=HIGH), 'col')  112 us
    psum x1, waiting for transfers between devices, local(): picked, spots = lax.psum((part_picked, part_spots), 'col')  72.7 us
    another operation x12, other arithmetic, ridge_fit(): factor = jnp.linalg.cholesky(gram + shift * ident)  49.6 us
    another operation x8, other arithmetic, ridge_fit(): return jax.scipy.linalg.cho_solve((factor, True), picked)  41.9 us
    dot_general x2, matrix products, omega_rows(): counted = jnp.dot(row_bits, col_bits, precision=HIGH)  33.3 us
    ppermute x9, starting transfers between devices, swapped(): return lax.ppermute(value, axis, pairs)  29.8 us
    psum x1, blocking collectives, local(): picked, spots = lax.psum((part_picked, part_spots), 'col')  25.2 us
    all_gather x1, blocking collectives, local(): distant_points = lax.all_gather(points, 'col', axis=1, tiled=True)  23.8 us
  transfers between devices with their start and end apart: 11, of which 8 were waited for; matrix products, arithmetic and copies ran while one was open for 8% of the time, Pallas kernels for 0%

commit v1 on v0

--- a/solution.py
+++ b/solution.py
@@ -69,7 +69,7 @@
     gram = jnp.dot(picked, picked.T, precision=HIGH)
     fitted = ridge_fit(picked, gram, leaf_rank)
     basis = jnp.dot(residue, fitted.T, precision=HIGH)
-    projected = lax.psum(jnp.dot(basis.T, own_omega, precision=HIGH), "col")
+    projected = jnp.sum(lax.all_gather(jnp.dot(basis.T, own_omega, precision=HIGH), "col"), axis=0)
     leaf_basis = basis.astype(jnp.bfloat16)
     span = width // col_count
     base = 0

time: 496 us -> 427 us (0.86)
  the two profiles are of different devices: /device:TPU:2 before, /device:TPU:8 now
where the time goes in v1:
time: 427 us; the launch traced here: 420 us
  waiting for transfers between devices  135 us (32%)
  other arithmetic  103 us (24%)
  blocking collectives  65.7 us (15%)
  matrix products  61.6 us (14%)
  starting transfers between devices  30.7 us (7%)
  between operations  20.6 us (5%)
  local copies, waits for them, and re-layouts  4.37 us (1%)
    psum x1, waiting for transfers between devices, local(): picked, spots = lax.psum((part_picked, part_spots), 'col')  108 us
    another operation x12, other arithmetic, ridge_fit(): factor = jnp.linalg.cholesky(gram + shift * ident)  49.6 us
    another operation x8, other arithmetic, ridge_fit(): return jax.scipy.linalg.cho_solve((factor, True), picked)  41.9 us
    dot_general x2, matrix products, omega_rows(): counted = jnp.dot(row_bits, col_bits, precision=HIGH)  33.3 us
    ppermute x9, starting transfers between devices, swapped(): return lax.ppermute(value, axis, pairs)  30 us
    psum x1, blocking collectives, local(): picked, spots = lax.psum((part_picked, part_spots), 'col')  27.4 us
    ppermute x9, waiting for transfers between devices, swapped(): return lax.ppermute(value, axis, pairs)  24.9 us
    all_gather x1, blocking collectives, local(): distant_points = lax.all_gather(points, 'col', axis=1, tiled=True)  23.8 us
  transfers between devices with their start and end apart: 11, of which 8 were waited for; matrix products, arithmetic and copies ran while one was open for 10% of the time, Pallas kernels for 0%

profile of v1, /device:TPU:8, one launch (start us, length us, event | category | flops | bytes accessed | tf_op | source)
XLA Modules:
  0.0 420.4 jit_solution(13305092889439046689)
XLA Ops:
  7.2 23.8 %all_gather.12 = f32[3,8192]{1,0:T(4,128)S(1)} all-gather(f32[3,512]{1,0:T(4,128)} %param.14), channel_id=1, replica_groups=mesh['leaf'=32,'col'=16] {'col'}, dimensions={1}, use_global_device_ids=true | all-gather | bytes 104448 | tf_op jit(solution)/shard_map/all_gather | solution.py:55
  31.0 0.8 fusion.198
  31.8 0.7 pad_add_fusion
  32.5 14.6 %all_gather.13 = s32[2,8192]{1,0:T(2,128)S(1)} all-gather(s32[2,512]{1,0:T(2,128)S(1)} %pad_add_fusion), channel_id=1, replica_groups=mesh['leaf'=32,'col'=16] {'col'}, dimensions={1}, use_global_device_ids=true | all-gather | bytes 69632 | tf_op jit(solution)/shard_map/all_gather | solution.py:56
  47.2 0.7 compare_reduce_fusion
  48.0 1.7 fusion.199
  50.4 0.8 fusion.165
  51.2 29.2 %multiply_convert_fusion = bf16[8192,512]{1,0:T(8,128)(2,1)S(1)} fusion(f32[8192]{0:T(1024)S(1)} %bitcast.152, s32[20]{0:T(128)} %constant.261.clone, s32[8192]{0:T(1024)S(1)} %bitcast.148, pred[8192]{0:T(1024)(128)(4,1)S(1)} %sign_compare_fusion, s32[512]{0:T(512)} %param.17, pred[512]{0:T(512)(128)(4,1)S(1)} %compare_reduce_fusion), kind=kOutput, calls=%fused_computation | convolution fusion | flops 1047515136 | bytes 8464976 | tf_op jit(solution)/shard_map/dot_general | solution.py:23
  80.4 6.7 %fusion.8 = f32[512,512]{1,0:T(8,128)S(1)} fusion(bf16[8192,512]{1,0:T(8,128)(2,1)S(1)} %multiply_convert_fusion, f32[8192]{0:T(1024)S(1)} %bitcast.150, f32[512]{0:T(512)S(1)} %bitcast.158, f32[8192]{0:T(1024)S(1)} %bitcast.151, f32[512]{0:T(512)S(1)} %bitcast.157, f32[8192]{0:T(1024)S(1)} %bitcast.149, f32[512]{0:T(512)S(1)} %bitcast.156, ...), kind=kOutput, calls=%fused_computation.10 | convolution fusion | flops 4337434624 | bytes 10065920 | tf_op jit(solution)/shard_map/dot_general | solution.py:59
  87.2 1.2 convolution_multiply_fusion.3
  88.4 0.7 all-gather.3.cloned.1.call-start
  89.8 4.1 fusion.54
  93.9 108.0 %all-reduce.2.cloned.1.call-done = f32[128,512]{1,0:T(8,128)} async-done(((f32[128,512]{1,0:T(8,128)}), f32[128,512]{1,0:T(8,128)}) %all-reduce.2.cloned.1.call-update) | async-done | bytes 262160 | tf_op jit(solution)/shard_map/psum | solution.py:68
  202.0 2.1 select_reduce_fusion.7
  204.9 11.7 %cholesky.74 = f32[128,128]{1,0:T(8,128)S(1)} custom-call(f32[128,128]{1,0:T(8,128)S(1)} %fusion.94), custom_call_target="Cholesky" | custom-call | tf_op jit(solution)/shard_map/jit(cholesky)/cholesky | solution.py:40
  217.9 9.8 %custom-call.10 = f32[1,128,128]{1,2,0:T(8,128)S(1)} custom-call(f32[1,128,128]{2,1,0:T(8,128)S(1)} %fusion.71), custom_call_target="InvertDiagBlocksLowerTriangular" | custom-call | tf_op jit(solution)/shard_map/jit(_cho_solve)/triangular_solve | solution.py:41
  227.8 1.4 fusion.92
  229.5 1.8 fusion.200
  231.3 1.8 fusion.9
  233.4 27.4 %psum.15 = f32[3,128]{1,0:T(4,128)S(1)} all-reduce(f32[3,128]{1,0:T(4,128)S(1)} %convolution_bitcast_fusion), channel_id=1, replica_groups=mesh['leaf'=32,'col'=16] {'col'}, use_global_device_ids=true, to_apply=%region_4.8 | all-reduce | flops 384 | bytes 3072 | tf_op jit(solution)/shard_map/psum | solution.py:68
  260.8 3.4 collective-permute-start.1
  271.9 4.7 %collective-permute-start.4 = (f32[3,128]{1,0:T(4,128)S(1)}, f32[3,128]{1,0:T(4,128)S(1)}, u32[]{:S(2)}, u32[]{:S(2)}) collective-permute-start(f32[3,128]{1,0:T(4,128)S(1)} %fusion.66), channel_id=1, source_target_pairs={{0,32},{16,48},{32,0},{48,16},{64,96},{80,112},{96,64},{112,80},{1... | collective-permute-start | bytes 4616 | tf_op jit(solution)/shard_map/ppermute | solution.py:16
  276.5 1.6 all-gather.3.cloned.1.call-done
  278.2 2.6 reduce_sum.30
  280.8 3.4 collective-permute-start.2
  284.2 2.5 collective-permute-start
  286.7 5.2 %collective-permute-done.2 = f32[128,512]{1,0:T(8,128)S(1)} collective-permute-done((f32[128,512]{1,0:T(8,128)S(1)}, f32[128,512]{1,0:T(8,128)S(1)}, u32[]{:S(2)}, u32[]{:S(2)}) %collective-permute-start.2) | collective-permute-done | bytes 262176 | tf_op jit(solution)/shard_map/ppermute | solution.py:16
  291.9 4.8 %collective-permute-done = f32[128,512]{1,0:T(8,128)S(1)} collective-permute-done((f32[128,512]{1,0:T(8,128)S(1)}, f32[128,512]{1,0:T(8,128)S(1)}, u32[]{:S(2)}, u32[]{:S(2)}) %collective-permute-start) | collective-permute-done | bytes 262176 | tf_op jit(solution)/shard_map/ppermute | solution.py:16
  298.1 1.0 select_reduce_fusion.6
  299.9 11.7 %cholesky.85 = f32[128,128]{1,0:T(8,128)S(1)} custom-call(f32[128,128]{1,0:T(8,128)S(1)} %fusion.89), custom_call_target="Cholesky" | custom-call | tf_op jit(solution)/shard_map/jit(cholesky)/cholesky | solution.py:40
  313.0 9.8 %custom-call.11 = f32[1,128,128]{1,2,0:T(8,128)S(1)} custom-call(f32[1,128,128]{2,1,0:T(8,128)S(1)} %fusion.72), custom_call_target="InvertDiagBlocksLowerTriangular" | custom-call | tf_op jit(solution)/shard_map/jit(_cho_solve)/triangular_solve | solution.py:41
  324.6 4.8 %collective-permute-start.5 = (f32[128,512]{1,0:T(8,128)S(1)}, f32[128,512]{1,0:T(8,128)S(1)}, u32[]{:S(2)}, u32[]{:S(2)}) collective-permute-start(f32[128,512]{1,0:T(8,128)S(1)} %fusion.25), channel_id=1, source_target_pairs={{0,32},{16,48},{32,0},{48,16},{64,96},{80,112},{96,64},{112,80},{1... | collective-permute-start | bytes 786440 | tf_op jit(solution)/shard_map/ppermute | solution.py:16
  329.5 2.5 collective-permute-start.3
  332.2 2.7 collective-permute-start.7
  334.9 1.8 collective-permute-done.5
  336.8 4.5 %collective-permute-done.3 = f32[128,512]{1,0:T(8,128)S(1)} collective-permute-done((f32[128,512]{1,0:T(8,128)S(1)}, f32[128,512]{1,0:T(8,128)S(1)}, u32[]{:S(2)}, u32[]{:S(2)}) %collective-permute-start.3) | collective-permute-done | bytes 262176 | tf_op jit(solution)/shard_map/ppermute | solution.py:16
  342.6 1.0 select_reduce_fusion.5
  344.4 11.7 %cholesky.96 = f32[128,128]{1,0:T(8,128)S(1)} custom-call(f32[128,128]{1,0:T(8,128)S(1)} %fusion.84), custom_call_target="Cholesky" | custom-call | tf_op jit(solution)/shard_map/jit(cholesky)/cholesky | solution.py:40
  357.5 9.8 %custom-call.12 = f32[1,128,128]{1,2,0:T(8,128)S(1)} custom-call(f32[1,128,128]{2,1,0:T(8,128)S(1)} %fusion.73), custom_call_target="InvertDiagBlocksLowerTriangular" | custom-call | tf_op jit(solution)/shard_map/jit(_cho_solve)/triangular_solve | solution.py:41
  369.1 2.4 collective-permute-start.8
  371.6 3.7 collective-permute-start.6
  375.3 4.9 %collective-permute-done.8 = f32[128,512]{1,0:T(8,128)S(1)} collective-permute-done((f32[128,512]{1,0:T(8,128)S(1)}, f32[128,512]{1,0:T(8,128)S(1)}, u32[]{:S(2)}, u32[]{:S(2)}) %collective-permute-start.8) | collective-permute-done | bytes 262176 | tf_op jit(solution)/shard_map/ppermute | solution.py:16
  380.3 3.6 collective-permute-done.6
  385.2 1.0 select_reduce_fusion.4
  387.1 11.7 %cholesky.107 = f32[128,128]{1,0:T(8,128)S(1)} custom-call(f32[128,128]{1,0:T(8,128)S(1)} %fusion.79), custom_call_target="Cholesky" | custom-call | tf_op jit(solution)/shard_map/jit(cholesky)/cholesky | solution.py:40
  400.1 9.8 %custom-call.13 = f32[1,128,128]{1,2,0:T(8,128)S(1)} custom-call(f32[1,128,128]{2,1,0:T(8,128)S(1)} %fusion.74), custom_call_target="InvertDiagBlocksLowerTriangular" | custom-call | tf_op jit(solution)/shard_map/jit(_cho_solve)/triangular_solve | solution.py:41
  411.8 0.7 dynamic_slice.64
  412.5 0.7 dynamic_slice.65
  (93 shorter events, 22.9 us)
Async XLA Ops:
  7.2 194.8 %all-reduce.2.cloned.1.call-start = ((), (), s32[]{:S(2)}) async-start(), calls=%async_computation | async-start | bytes 524288 | tf_op jit(solution)/shard_map/psum | solution.py:68
  51.2 29.2 %copy-start.5 = (bf16[512,512]{1,0:T(8,128)(2,1)S(1)}, bf16[512,512]{1,0:T(8,128)(2,1)}, u32[]{:S(2)}) copy-start(bf16[512,512]{1,0:T(8,128)(2,1)} %param.18) | copy-start | bytes 1572868
  80.4 9.4 %copy-start.2 = (s32[512]{0:T(512)S(1)}, s32[512]{0:T(512)}, u32[]{:S(2)}) copy-start(s32[512]{0:T(512)} %param.15) | copy-start | bytes 6148
  80.4 9.4 %copy-start.4 = (s32[512]{0:T(512)S(1)}, s32[512]{0:T(512)}, u32[]{:S(2)}) copy-start(s32[512]{0:T(512)} %param.17) | copy-start | bytes 6148
  80.4 9.4 %copy-start.6 = (s32[20]{0:T(128)S(1)}, s32[20]{0:T(128)}, u32[]{:S(2)}) copy-start(s32[20]{0:T(128)} %constant.261.clone) | copy-start | bytes 244
  80.4 13.5 %copy-start.3 = (s32[512]{0:T(512)S(1)}, s32[512]{0:T(512)}, u32[]{:S(2)}) copy-start(s32[512]{0:T(512)} %param.16) | copy-start | bytes 6148
  87.2 146.0 %copy-start.1 = (f32[3,512]{1,0:T(4,128)S(1)}, f32[3,512]{1,0:T(4,128)}, u32[]{:S(2)}) copy-start(f32[3,512]{1,0:T(4,128)} %param.14) | copy-start | bytes 18436
  88.4 189.8 %all-gather.3.cloned.1.call-start = ((), (), s32[]{:S(2)}) async-start(), calls=%async_computation.1 | async-start | bytes 4456448 | tf_op jit(solution)/shard_map/all_gather | solution.py:72
  202.0 82.3 %copy-start = (f32[128,512]{1,0:T(8,128)S(1)}, f32[128,512]{1,0:T(8,128)}, u32[]{:S(2)}) copy-start(f32[128,512]{1,0:T(8,128)} %all-reduce.2.cloned.1.call-done) | copy-start | bytes 786436
  260.8 10.9 %collective-permute-start.1 = (f32[3,128]{1,0:T(4,128)S(1)}, f32[3,128]{1,0:T(4,128)S(1)}, u32[]{:S(2)}, u32[]{:S(2)}) collective-permute-start(f32[3,128]{1,0:T(4,128)S(1)} %psum.15), channel_id=1, source_target_pairs={{0,16},{16,0},{32,48},{48,32},{64,80},{80,64},{96,112},{112,96},{1... | collective-permute-start | bytes 4616 | tf_op jit(solution)/shard_map/ppermute | solution.py:16
  271.9 14.8 %collective-permute-start.4 = (f32[3,128]{1,0:T(4,128)S(1)}, f32[3,128]{1,0:T(4,128)S(1)}, u32[]{:S(2)}, u32[]{:S(2)}) collective-permute-start(f32[3,128]{1,0:T(4,128)S(1)} %fusion.66), channel_id=1, source_target_pairs={{0,32},{16,48},{32,0},{48,16},{64,96},{80,112},{96,64},{112,80},{1... | collective-permute-start | bytes 4616 | tf_op jit(solution)/shard_map/ppermute | solution.py:16
  280.8 11.1 %collective-permute-start.2 = (f32[128,512]{1,0:T(8,128)S(1)}, f32[128,512]{1,0:T(8,128)S(1)}, u32[]{:S(2)}, u32[]{:S(2)}) collective-permute-start(f32[128,512]{1,0:T(8,128)S(1)} %reduce_sum.30), channel_id=1, source_target_pairs={{0,16},{16,0},{32,48},{48,32},{64,80},{80,64},{96,112},{112,96},{1... | collective-permute-start | bytes 786440 | tf_op jit(solution)/shard_map/ppermute | solution.py:16
  284.2 12.5 %collective-permute-start = (f32[128,512]{1,0:T(8,128)S(1)}, f32[128,512]{1,0:T(8,128)S(1)}, u32[]{:S(2)}, u32[]{:S(2)}) collective-permute-start(f32[128,512]{1,0:T(8,128)S(1)} %copy-done), channel_id=1, source_target_pairs={{0,16},{16,0},{32,48},{48,32},{64,80},{80,64},{96,112},{112,96},{1... | collective-permute-start | bytes 786440 | tf_op jit(solution)/shard_map/ppermute | solution.py:16
  324.6 12.1 %collective-permute-start.5 = (f32[128,512]{1,0:T(8,128)S(1)}, f32[128,512]{1,0:T(8,128)S(1)}, u32[]{:S(2)}, u32[]{:S(2)}) collective-permute-start(f32[128,512]{1,0:T(8,128)S(1)} %fusion.25), channel_id=1, source_target_pairs={{0,32},{16,48},{32,0},{48,16},{64,96},{80,112},{96,64},{112,80},{1... | collective-permute-start | bytes 786440 | tf_op jit(solution)/shard_map/ppermute | solution.py:16
  329.5 11.8 %collective-permute-start.3 = (f32[128,512]{1,0:T(8,128)S(1)}, f32[128,512]{1,0:T(8,128)S(1)}, u32[]{:S(2)}, u32[]{:S(2)}) collective-permute-start(f32[128,512]{1,0:T(8,128)S(1)} %convolution_multiply_fusion.2), channel_id=1, source_target_pairs={{0,32},{16,48},{32,0},{48,16},{64,96},{80,112},{96,64},{112,80},{1... | collective-permute-start | bytes 786440 | tf_op jit(solution)/shard_map/ppermute | solution.py:16
  332.2 39.3 %collective-permute-start.7 = (f32[3,128]{1,0:T(4,128)S(1)}, f32[3,128]{1,0:T(4,128)S(1)}, u32[]{:S(2)}, u32[]{:S(2)}) collective-permute-start(f32[3,128]{1,0:T(4,128)S(1)} %fusion.67), channel_id=1, source_target_pairs={{0,64},{16,80},{32,96},{48,112},{64,0},{80,16},{96,32},{112,48},{1... | collective-permute-start | bytes 4616 | tf_op jit(solution)/shard_map/ppermute | solution.py:16
  369.1 11.1 %collective-permute-start.8 = (f32[128,512]{1,0:T(8,128)S(1)}, f32[128,512]{1,0:T(8,128)S(1)}, u32[]{:S(2)}, u32[]{:S(2)}) collective-permute-start(f32[128,512]{1,0:T(8,128)S(1)} %fusion.29), channel_id=1, source_target_pairs={{0,64},{16,80},{32,96},{48,112},{64,0},{80,16},{96,32},{112,48},{1... | collective-permute-start | bytes 786440 | tf_op jit(solution)/shard_map/ppermute | solution.py:16
  371.6 12.3 %collective-permute-start.6 = (f32[128,512]{1,0:T(8,128)S(1)}, f32[128,512]{1,0:T(8,128)S(1)}, u32[]{:S(2)}, u32[]{:S(2)}) collective-permute-start(f32[128,512]{1,0:T(8,128)S(1)} %convolution_multiply_fusion.1), channel_id=1, source_target_pairs={{0,64},{16,80},{32,96},{48,112},{64,0},{80,16},{96,32},{112,48},{1... | collective-permute-start | bytes 786440 | tf_op jit(solution)/shard_map/ppermute | solution.py:16
Sparse Core Ops, SparseCore 0:
  88.5 113.3 all-reduce.1
  233.3 44.8 all-gather.2
